TPU v7x, 32 devices: a whole 2x2x4 slice. The times are simulated.
32 devices in a mesh: groups: 2 (over y), sub: 16 (over z, x, core).
Axes of the slice: x: 2, y: 2, z: 4, core: 2. Of those that a mesh axis runs over, the one named last changes fastest.
Arguments:
- modes: bfloat16 [65536, 512], P(('groups', 'sub')), parts along dimension 0, may hold values from -0.5 to 0.5
- eigenvalues: float32 [32, 512], P(('groups', 'sub')), parts along dimension 0, may hold values from 2 to 20
- sub_size: int32 [32], P(('groups', 'sub')), parts along dimension 0, may hold values from 1024 to 2048
- row_offset: int32 [1024, 128], P(('groups', 'sub')), parts along dimension 0, may hold values from 0 to 1023
- stiff_coupling: bfloat16 [1024, 128, 128], P(('groups', 'sub')), parts along dimension 0, may hold values from -0.29882812 to 0.29882812
- iface_offset: int32 [1024], P(('groups', 'sub')), parts along dimension 0, may hold values from 0 to 6
- stiff_iface: float32 [32, 128, 128], P(('groups', 'sub')), parts along dimension 0, may hold values from -18 to 18
- lumped_mass: float32 [32, 128], P(('groups', 'sub')), parts along dimension 0, may hold values from 0.5 to 5
Outputs:
- reduced: float32 [32, 128, 128], P(('groups', 'sub')), parts along dimension 0
- factor: float32 [32, 128, 128], P(('groups', 'sub')), parts along dimension 0
- coupled: bfloat16 [1024, 512, 128], P(('groups', 'sub')), parts along dimension 0
There are 2 independent parts, one for each index of `groups`. A program takes and returns all parts, laid end to end along the dimension named above; each array names one. Nothing has to cross between parts.
Inputs may be any that keep to these rules, and one draw needn't show every extreme that they name: Block b of substructure s belongs to interface (s + iface_offset[b] - 3) mod 16, so a substructure's interfaces lie within 3 places of it in substructure order.
All inputs are finite; a program needn't handle non-finite values.
Results may differ from a plain program's by a relative error of at most 0.001.
The roundings to bfloat16 on the way count: a program that leaves them out, or rounds other values in their place, can miss the bound.
Values sent between devices are 32-bit elements; how exact they have to be, the bound alone decides.
A program may use at most 64 MiB of HBM per device.

v0:
```python
import jax
import jax.numpy as jnp
from jax import lax
from jax.sharding import PartitionSpec as P

REACH = 3


def passed_along(x, axis, by):
    length = lax.axis_size(axis)
    return lax.ppermute(x, axis, [(i, (i + by) % length) for i in range(length)])


def per_device(
    modes, eigenvalues, sub_size, row_offset, stiff_coupling, iface_offset, stiff_iface, lumped_mass
):
    iface_width = stiff_coupling.shape[2]
    picked_rows = sub_size[0] - 1 - row_offset
    picked = jnp.take(modes, picked_rows, axis=0)
    projected = jnp.einsum(
        "brm,bri->bmi", picked, stiff_coupling, preferred_element_type=jnp.float32
    ).astype(jnp.bfloat16)
    widened = projected.astype(jnp.float32)
    inverse = 1.0 / eigenvalues[0]
    stiff_part = jnp.einsum(
        "bmi,bmj->bij", widened * inverse[None, :, None], widened, precision=lax.Precision.HIGHEST
    )
    mass_part = jnp.einsum(
        "bmi,bmj->bij",
        widened * (inverse * inverse)[None, :, None],
        widened,
        precision=lax.Precision.HIGHEST,
    )
    stacked = jnp.stack([stiff_part, mass_part], axis=1)
    shifted = iface_offset - REACH
    distances = jnp.arange(-REACH, REACH + 1, dtype=jnp.int32)
    selector = (distances[:, None] == shifted[None, :]).astype(jnp.float32)
    by_offset = jnp.einsum("jb,bkxy->jkxy", selector, stacked, precision=lax.Precision.HIGHEST)
    summed = by_offset[REACH]
    for distance in range(-REACH, REACH + 1):
        if distance != 0:
            summed = summed + passed_along(by_offset[distance + REACH], "sub", distance)
    identity = jnp.eye(iface_width, dtype=jnp.float32)
    reduced = stiff_iface - summed[0][None]
    mass_matrix = summed[1][None] + lumped_mass[:, :, None] * identity[None]
    factor = jnp.linalg.cholesky(mass_matrix)
    own_inverse = lax.linalg.triangular_solve(factor[0], identity, left_side=True, lower=True)
    pieces = []
    for distance in range(-REACH, REACH + 1):
        if distance == 0:
            pieces.append(own_inverse)
        else:
            pieces.append(passed_along(own_inverse, "sub", -distance))
    nearby = jnp.stack(pieces)
    chosen = jnp.take(nearby, iface_offset, axis=0)
    solved = jnp.einsum("bmi,bji->bmj", widened, chosen, precision=lax.Precision.HIGHEST)
    return (reduced, factor, solved.astype(jnp.bfloat16))


def solution(mesh):
    placed = (
        P(("groups", "sub"), None),
        P(("groups", "sub"), None),
        P(("groups", "sub")),
        P(("groups", "sub"), None),
        P(("groups", "sub"), None, None),
        P(("groups", "sub")),
        P(("groups", "sub"), None, None),
        P(("groups", "sub"), None),
    )
    return jax.shard_map(
        per_device,
        mesh=mesh,
        in_specs=placed,
        out_specs=(
            P(("groups", "sub"), None, None),
            P(("groups", "sub"), None, None),
            P(("groups", "sub"), None, None),
        ),
        check_vma=False,
    )
```

profile of v0, /device:TPU:0, one launch (start us, length us, event | category | flops | bytes accessed | tf_op | source)
XLA Modules:
  0.0 114.1 jit_solution(12641995247238551872)
XLA Ops:
  1.4 0.7 bitcast_clamp_fusion
  2.2 0.7 compare_and_fusion
  2.9 17.3 %gather_fusion = bf16[4096,512]{1,0:T(8,128)(2,1)} fusion(bf16[2048,512]{1,0:T(8,128)(2,1)S(1)} %copy-done, s32[4096]{0:T(1024)S(1)} %bitcast_clamp_fusion), kind=kCustom, calls=%fused_computation | custom fusion | bytes 8404992 | tf_op jit(solution)/shard_map/jit(_take)/gather | solution.py:19
  20.3 6.5 %copy.11 = bf16[32,128,512]{1,2,0:T(8,128)(2,1)} copy(bf16[32,128,512]{2,1,0:T(8,128)(2,1)} %bitcast.61) | data formatting | bytes 8388608 | tf_op jit(solution)/shard_map/jit(_take)/gather | solution.py:19
  26.8 3.4 %fusion.9 = bf16[32,512,128]{2,1,0:T(8,128)(2,1)S(1)} fusion(bf16[32,128,128]{2,1,0:T(8,128)(2,1)S(1)} %copy-done.5, bf16[32,128,512]{1,2,0:T(8,128)(2,1)} %copy.11, pred[32,128]{1,0:T(8,128)(4,1)S(1)} %compare_and_fusion), kind=kOutput, calls=%fused_computation.15 | convolution fusion | flops 541065216 | bytes 9441280 | tf_op jit(solution)/shard_map/brm,bri->bmi/dot_general | solution.py:20
  30.3 7.0 %fusion.15 = f32[32,1,128,128]{3,2,0,1:T(8,128)S(1)} fusion(bf16[32,512,128]{2,1,0:T(8,128)(2,1)S(1)} %fusion.9, f32[512]{0:T(512)S(1)} %bitcast.71), kind=kOutput, calls=%fused_computation.19 | convolution fusion | flops 3225419776 | bytes 6293504 | tf_op jit(solution)/shard_map/bmi,bmj->bij/dot_general | solution.py:25
  37.3 7.2 %fusion.14 = f32[32,1,128,128]{3,2,0,1:T(8,128)S(1)} fusion(bf16[32,512,128]{2,1,0:T(8,128)(2,1)S(1)} %fusion.9, f32[512]{0:T(512)S(1)} %mul.35), kind=kOutput, calls=%fused_computation.18 | convolution fusion | flops 3225419776 | bytes 6293504 | tf_op jit(solution)/shard_map/bmi,bmj->bij/dot_general | solution.py:28
  44.6 0.3 pad_maximum_fusion
  44.9 3.9 %fusion.2 = f32[7,2,128,128]{3,0,2,1:T(8,128)S(1)} fusion(f32[32,2,128,128]{3,2,0,1:T(8,128)S(1)} %pad_maximum_fusion, s32[32]{0:T(128)S(1)} %get-tuple-element.15, s32[7]{0:T(128)S(1)} %iota_add_fusion), kind=kOutput, calls=%fused_computation.7 | convolution fusion | flops 88080608 | bytes 5111964 | tf_op jit(solution)/shard_map/jb,bkxy->jkxy/dot_general | solution.py:38
  48.8 0.7 fusion.28
  49.5 4.6 %collective-permute-start = (f32[2,128,128]{2,1,0:T(8,128)S(1)}, f32[2,128,128]{2,1,0:T(8,128)S(1)}, u32[]{:S(2)}, u32[]{:S(2)}) collective-permute-start(f32[2,128,128]{2,1,0:T(8,128)S(1)} %bitcast.68), channel_id=1, source_target_pairs={{0,13},{1,14},{2,15},{3,0},{4,1},{5,2},{6,3},{7,4},{8,5},{9,6},{10... | collective-permute-start | bytes 393224 | tf_op jit(solution)/shard_map/ppermute | solution.py:11
  54.1 1.6 %collective-permute-start.1 = (f32[2,128,128]{2,1,0:T(8,128)S(1)}, f32[2,128,128]{2,1,0:T(8,128)S(1)}, u32[]{:S(2)}, u32[]{:S(2)}) collective-permute-start(f32[2,128,128]{2,1,0:T(8,128)S(1)} %bitcast.67), channel_id=1, source_target_pairs={{0,14},{1,15},{2,0},{3,1},{4,2},{5,3},{6,4},{7,5},{8,6},{9,7},{10,... | collective-permute-start | bytes 393224 | tf_op jit(solution)/shard_map/ppermute | solution.py:11
  55.7 1.3 %collective-permute-start.2 = (f32[2,128,128]{2,1,0:T(8,128)S(1)}, f32[2,128,128]{2,1,0:T(8,128)S(1)}, u32[]{:S(2)}, u32[]{:S(2)}) collective-permute-start(f32[2,128,128]{2,1,0:T(8,128)S(1)} %bitcast.66), channel_id=1, source_target_pairs={{0,15},{1,0},{2,1},{3,2},{4,3},{5,4},{6,5},{7,6},{8,7},{9,8},{10,9... | collective-permute-start | bytes 393224 | tf_op jit(solution)/shard_map/ppermute | solution.py:11
  56.9 0.6 collective-permute-start.4
  57.6 2.1 %collective-permute-start.5 = (f32[2,128,128]{2,1,0:T(8,128)S(1)}, f32[2,128,128]{2,1,0:T(8,128)S(1)}, u32[]{:S(2)}, u32[]{:S(2)}) collective-permute-start(f32[2,128,128]{2,1,0:T(8,128)S(1)} %bitcast.63), channel_id=1, source_target_pairs={{0,3},{1,4},{2,5},{3,6},{4,7},{5,8},{6,9},{7,10},{8,11},{9,12},{10... | collective-permute-start | bytes 393224 | tf_op jit(solution)/shard_map/ppermute | solution.py:11
  59.9 2.9 %collective-permute-done.2 = f32[2,128,128]{2,1,0:T(8,128)S(1)} collective-permute-done((f32[2,128,128]{2,1,0:T(8,128)S(1)}, f32[2,128,128]{2,1,0:T(8,128)S(1)}, u32[]{:S(2)}, u32[]{:S(2)}) %collective-permute-start.2) | collective-permute-done | bytes 131104 | tf_op jit(solution)/shard_map/ppermute | solution.py:11
  62.7 2.1 %collective-permute-done.3 = f32[2,128,128]{2,1,0:T(8,128)S(1)} collective-permute-done((f32[2,128,128]{2,1,0:T(8,128)S(1)}, f32[2,128,128]{2,1,0:T(8,128)S(1)}, u32[]{:S(2)}, u32[]{:S(2)}) %collective-permute-start.3) | collective-permute-done | bytes 131104 | tf_op jit(solution)/shard_map/ppermute | solution.py:11
  64.8 1.2 %collective-permute-done.4 = f32[2,128,128]{2,1,0:T(8,128)S(1)} collective-permute-done((f32[2,128,128]{2,1,0:T(8,128)S(1)}, f32[2,128,128]{2,1,0:T(8,128)S(1)}, u32[]{:S(2)}, u32[]{:S(2)}) %collective-permute-start.4) | collective-permute-done | bytes 131104 | tf_op jit(solution)/shard_map/ppermute | solution.py:11
  66.1 0.6 slice_add_fusion
  66.9 11.7 %custom-call.7 = f32[1,128,128]{2,1,0:T(8,128)S(1)} custom-call(f32[1,128,128]{2,1,0:T(8,128)S(1)} %fusion.20), custom_call_target="Cholesky" | custom-call | tf_op jit(solution)/shard_map/jit(cholesky)/cholesky | solution.py:46
  78.6 0.6 compare_reduce_fusion
  79.3 1.3 %fusion.21 = (f32[1,128,128]{2,1,0:T(8,128)S(1)}, f32[1,128,128]{2,1,0:T(8,128)}) fusion(f32[1,128,128]{2,1,0:T(8,128)S(1)} %custom-call.7, pred[]{:T(512)} %compare_reduce_fusion), kind=kLoop, calls=%fused_computation.41 | loop fusion | flops 65536 | bytes 196609 | tf_op jit(solution)/shard_map/triangular_solve | solution.py:47
  80.5 9.8 %custom-call.8 = f32[1,128,128]{1,2,0:T(8,128)S(1)} custom-call(f32[1,128,128]{2,1,0:T(8,128)S(1)} %get-tuple-element.3), custom_call_target="InvertDiagBlocksLowerTriangular" | custom-call | tf_op jit(solution)/shard_map/triangular_solve | solution.py:47
  90.6 2.2 %collective-permute-start.6 = (f32[128,128]{1,0:T(8,128)S(1)}, f32[128,128]{1,0:T(8,128)S(1)}, u32[]{:S(2)}, u32[]{:S(2)}) collective-permute-start(f32[128,128]{1,0:T(8,128)S(1)} %fusion.18), channel_id=1, source_target_pairs={{0,3},{1,4},{2,5},{3,6},{4,7},{5,8},{6,9},{7,10},{8,11},{9,12},{10... | collective-permute-start | bytes 196616 | tf_op jit(solution)/shard_map/ppermute | solution.py:11
  92.8 2.1 %collective-permute-start.7 = (f32[128,128]{1,0:T(8,128)S(1)}, f32[128,128]{1,0:T(8,128)S(1)}, u32[]{:S(2)}, u32[]{:S(2)}) collective-permute-start(f32[128,128]{1,0:T(8,128)S(1)} %fusion.18), channel_id=1, source_target_pairs={{0,2},{1,3},{2,4},{3,5},{4,6},{5,7},{6,8},{7,9},{8,10},{9,11},{10,... | collective-permute-start | bytes 196616 | tf_op jit(solution)/shard_map/ppermute | solution.py:11
  94.9 4.4 %collective-permute-start.9 = (f32[128,128]{1,0:T(8,128)S(1)}, f32[128,128]{1,0:T(8,128)S(1)}, u32[]{:S(2)}, u32[]{:S(2)}) collective-permute-start(f32[128,128]{1,0:T(8,128)S(1)} %fusion.18), channel_id=1, source_target_pairs={{0,15},{1,0},{2,1},{3,2},{4,3},{5,4},{6,5},{7,6},{8,7},{9,8},{10,9... | collective-permute-start | bytes 196616 | tf_op jit(solution)/shard_map/ppermute | solution.py:11
  99.6 1.0 collective-permute-start.11
  100.5 1.5 %collective-permute-done.7 = f32[128,128]{1,0:T(8,128)S(1)} collective-permute-done((f32[128,128]{1,0:T(8,128)S(1)}, f32[128,128]{1,0:T(8,128)S(1)}, u32[]{:S(2)}, u32[]{:S(2)}) %collective-permute-start.7) | collective-permute-done | bytes 65568 | tf_op jit(solution)/shard_map/ppermute | solution.py:11
  102.0 0.6 collective-permute-done.8
  102.7 1.4 %collective-permute-done.10 = f32[128,128]{1,0:T(8,128)S(1)} collective-permute-done((f32[128,128]{1,0:T(8,128)S(1)}, f32[128,128]{1,0:T(8,128)S(1)}, u32[]{:S(2)}, u32[]{:S(2)}) %collective-permute-start.10) | collective-permute-done | bytes 65568 | tf_op jit(solution)/shard_map/ppermute | solution.py:11
  104.1 2.0 %gather_fusion.1 = f32[32,128,128]{2,1,0:T(8,128)} fusion(f32[7,128,128]{2,1,0:T(8,128)S(1)} %bitcast_dynamic-update-slice_fusion, s32[1024]{0:T(1024)S(1)} %pad_clamp_fusion), kind=kCustom, calls=%fused_computation.1 | custom fusion | bytes 4194432 | tf_op jit(solution)/shard_map/jit(_take)/gather | solution.py:55
  106.1 8.0 %convolution_convert_fusion = bf16[32,512,128]{2,1,0:T(8,128)(2,1)} fusion(bf16[32,512,128]{2,1,0:T(8,128)(2,1)} %copy-done.1, f32[32,128,128]{2,1,0:T(8,128)} %gather_fusion.1, pred[32]{0:T(512)(128)(4,1)S(1)} %compare_and_fusion.1), kind=kOutput, calls=%fused_computation.14 | convolution fusion | flops 3223846912 | bytes 10485792 | tf_op jit(solution)/shard_map/bmi,bji->bmj/dot_general | solution.py:56
  (41 shorter events, 1.0 us)
Async XLA Ops:
  0.6 2.3 %copy-start = (bf16[2048,512]{1,0:T(8,128)(2,1)S(1)}, bf16[2048,512]{1,0:T(8,128)(2,1)}, u32[]{:S(2)}) copy-start(bf16[2048,512]{1,0:T(8,128)(2,1)} %param.8) | copy-start | bytes 6291460
  20.2 6.5 %copy-start.3 = (f32[1,512]{1,0:T(1,128)S(1)}, f32[1,512]{1,0:T(1,128)}, u32[]{:S(2)}) copy-start(f32[1,512]{1,0:T(1,128)} %param.9) | copy-start | bytes 6148
  20.3 6.5 %copy-start.5 = (bf16[32,128,128]{2,1,0:T(8,128)(2,1)S(1)}, bf16[32,128,128]{2,1,0:T(8,128)(2,1)}, u32[]{:S(2)}) copy-start(bf16[32,128,128]{2,1,0:T(8,128)(2,1)} %param.12) | copy-start | bytes 3145732
  30.3 7.1 %copy-start.1 = (bf16[32,512,128]{2,1,0:T(8,128)(2,1)}, bf16[32,512,128]{2,1,0:T(8,128)(2,1)S(1)}, u32[]{:S(2)}) copy-start(bf16[32,512,128]{2,1,0:T(8,128)(2,1)S(1)} %fusion.9) | copy-start | bytes 12582916
  37.3 7.2 %copy-start.6 = (s32[32]{0:T(128)S(1)}, s32[32]{0:T(128)}, u32[]{:S(2)}) copy-start(s32[32]{0:T(128)} %param.13) | copy-start | bytes 388
  44.8 21.2 %copy-start.2 = (f32[1,128,128]{2,1,0:T(8,128)S(1)}, f32[1,128,128]{2,1,0:T(8,128)}, u32[]{:S(2)}) copy-start(f32[1,128,128]{2,1,0:T(8,128)} %param.14) | copy-start | bytes 196612
  44.9 21.2 %copy-start.4 = (f32[1,128]{1,0:T(1,128)S(1)}, f32[1,128]{1,0:T(1,128)}, u32[]{:S(2)}) copy-start(f32[1,128]{1,0:T(1,128)} %param.15) | copy-start | bytes 1540
  49.5 8.1 %collective-permute-start = (f32[2,128,128]{2,1,0:T(8,128)S(1)}, f32[2,128,128]{2,1,0:T(8,128)S(1)}, u32[]{:S(2)}, u32[]{:S(2)}) collective-permute-start(f32[2,128,128]{2,1,0:T(8,128)S(1)} %bitcast.68), channel_id=1, source_target_pairs={{0,13},{1,14},{2,15},{3,0},{4,1},{5,2},{6,3},{7,4},{8,5},{9,6},{10... | collective-permute-start | bytes 393224 | tf_op jit(solution)/shard_map/ppermute | solution.py:11
  54.1 5.8 %collective-permute-start.1 = (f32[2,128,128]{2,1,0:T(8,128)S(1)}, f32[2,128,128]{2,1,0:T(8,128)S(1)}, u32[]{:S(2)}, u32[]{:S(2)}) collective-permute-start(f32[2,128,128]{2,1,0:T(8,128)S(1)} %bitcast.67), channel_id=1, source_target_pairs={{0,14},{1,15},{2,0},{3,1},{4,2},{5,3},{6,4},{7,5},{8,6},{9,7},{10,... | collective-permute-start | bytes 393224 | tf_op jit(solution)/shard_map/ppermute | solution.py:11
  55.7 7.1 %collective-permute-start.2 = (f32[2,128,128]{2,1,0:T(8,128)S(1)}, f32[2,128,128]{2,1,0:T(8,128)S(1)}, u32[]{:S(2)}, u32[]{:S(2)}) collective-permute-start(f32[2,128,128]{2,1,0:T(8,128)S(1)} %bitcast.66), channel_id=1, source_target_pairs={{0,15},{1,0},{2,1},{3,2},{4,3},{5,4},{6,5},{7,6},{8,7},{9,8},{10,9... | collective-permute-start | bytes 393224 | tf_op jit(solution)/shard_map/ppermute | solution.py:11
  56.9 7.9 %collective-permute-start.3 = (f32[2,128,128]{2,1,0:T(8,128)S(1)}, f32[2,128,128]{2,1,0:T(8,128)S(1)}, u32[]{:S(2)}, u32[]{:S(2)}) collective-permute-start(f32[2,128,128]{2,1,0:T(8,128)S(1)} %bitcast.65), channel_id=1, source_target_pairs={{0,1},{1,2},{2,3},{3,4},{4,5},{5,6},{6,7},{7,8},{8,9},{9,10},{10,1... | collective-permute-start | bytes 393224 | tf_op jit(solution)/shard_map/ppermute | solution.py:11
  56.9 9.1 %collective-permute-start.4 = (f32[2,128,128]{2,1,0:T(8,128)S(1)}, f32[2,128,128]{2,1,0:T(8,128)S(1)}, u32[]{:S(2)}, u32[]{:S(2)}) collective-permute-start(f32[2,128,128]{2,1,0:T(8,128)S(1)} %bitcast.64), channel_id=1, source_target_pairs={{0,2},{1,3},{2,4},{3,5},{4,6},{5,7},{6,8},{7,9},{8,10},{9,11},{10,... | collective-permute-start | bytes 393224 | tf_op jit(solution)/shard_map/ppermute | solution.py:11
  57.6 8.4 %collective-permute-start.5 = (f32[2,128,128]{2,1,0:T(8,128)S(1)}, f32[2,128,128]{2,1,0:T(8,128)S(1)}, u32[]{:S(2)}, u32[]{:S(2)}) collective-permute-start(f32[2,128,128]{2,1,0:T(8,128)S(1)} %bitcast.63), channel_id=1, source_target_pairs={{0,3},{1,4},{2,5},{3,6},{4,7},{5,8},{6,9},{7,10},{8,11},{9,12},{10... | collective-permute-start | bytes 393224 | tf_op jit(solution)/shard_map/ppermute | solution.py:11
  90.6 9.0 %collective-permute-start.6 = (f32[128,128]{1,0:T(8,128)S(1)}, f32[128,128]{1,0:T(8,128)S(1)}, u32[]{:S(2)}, u32[]{:S(2)}) collective-permute-start(f32[128,128]{1,0:T(8,128)S(1)} %fusion.18), channel_id=1, source_target_pairs={{0,3},{1,4},{2,5},{3,6},{4,7},{5,8},{6,9},{7,10},{8,11},{9,12},{10... | collective-permute-start | bytes 196616 | tf_op jit(solution)/shard_map/ppermute | solution.py:11
  92.8 9.2 %collective-permute-start.7 = (f32[128,128]{1,0:T(8,128)S(1)}, f32[128,128]{1,0:T(8,128)S(1)}, u32[]{:S(2)}, u32[]{:S(2)}) collective-permute-start(f32[128,128]{1,0:T(8,128)S(1)} %fusion.18), channel_id=1, source_target_pairs={{0,2},{1,3},{2,4},{3,5},{4,6},{5,7},{6,8},{7,9},{8,10},{9,11},{10,... | collective-permute-start | bytes 196616 | tf_op jit(solution)/shard_map/ppermute | solution.py:11
  94.9 7.8 %collective-permute-start.8 = (f32[128,128]{1,0:T(8,128)S(1)}, f32[128,128]{1,0:T(8,128)S(1)}, u32[]{:S(2)}, u32[]{:S(2)}) collective-permute-start(f32[128,128]{1,0:T(8,128)S(1)} %fusion.18), channel_id=1, source_target_pairs={{0,1},{1,2},{2,3},{3,4},{4,5},{5,6},{6,7},{7,8},{8,9},{9,10},{10,1... | collective-permute-start | bytes 196616 | tf_op jit(solution)/shard_map/ppermute | solution.py:11
  94.9 7.8 %collective-permute-start.9 = (f32[128,128]{1,0:T(8,128)S(1)}, f32[128,128]{1,0:T(8,128)S(1)}, u32[]{:S(2)}, u32[]{:S(2)}) collective-permute-start(f32[128,128]{1,0:T(8,128)S(1)} %fusion.18), channel_id=1, source_target_pairs={{0,15},{1,0},{2,1},{3,2},{4,3},{5,4},{6,5},{7,6},{8,7},{9,8},{10,9... | collective-permute-start | bytes 196616 | tf_op jit(solution)/shard_map/ppermute | solution.py:11
  99.4 4.7 %collective-permute-start.10 = (f32[128,128]{1,0:T(8,128)S(1)}, f32[128,128]{1,0:T(8,128)S(1)}, u32[]{:S(2)}, u32[]{:S(2)}) collective-permute-start(f32[128,128]{1,0:T(8,128)S(1)} %fusion.18), channel_id=1, source_target_pairs={{0,14},{1,15},{2,0},{3,1},{4,2},{5,3},{6,4},{7,5},{8,6},{9,7},{10,... | collective-permute-start | bytes 196616 | tf_op jit(solution)/shard_map/ppermute | solution.py:11
  99.6 4.5 %collective-permute-start.11 = (f32[128,128]{1,0:T(8,128)S(1)}, f32[128,128]{1,0:T(8,128)S(1)}, u32[]{:S(2)}, u32[]{:S(2)}) collective-permute-start(f32[128,128]{1,0:T(8,128)S(1)} %fusion.18), channel_id=1, source_target_pairs={{0,13},{1,14},{2,15},{3,0},{4,1},{5,2},{6,3},{7,4},{8,5},{9,6},{10... | collective-permute-start | bytes 196616 | tf_op jit(solution)/shard_map/ppermute | solution.py:11
where the time goes:
time: 114 us
  matrix products  29.8 us (26%)
  local copies, waits for them, and re-layouts  26.8 us (24%)
  other arithmetic  25.9 us (23%)
  starting transfers between devices  20.1 us (18%)
  waiting for transfers between devices  9.81 us (9%)
  between operations  1.64 us (1%)
    gather x2, local copies, waits for them, and re-layouts, per_device(): picked = jnp.take(modes, picked_rows, axis=0)  23.9 us
    ppermute x12, starting transfers between devices, passed_along(): lax.ppermute(x, axis, [(i, (i + by) % length) for i in range(length)])  20.1 us
    another operation x3, other arithmetic, per_device(): factor = jnp.linalg.cholesky(mass_matrix)  12.4 us
    another operation x2, other arithmetic, per_device(): lax.linalg.triangular_solve(factor[0], identity, left_side=True, lower=True)  11.1 us
    ppermute x12, waiting for transfers between devices, passed_along(): lax.ppermute(x, axis, [(i, (i + by) % length) for i in range(length)])  9.81 us
    dot_general x1, matrix products, per_device(): jnp.einsum('bmi,bji->bmj', widened, chosen, precision=lax.Precision.HIGHEST)  7.97 us
    dot_general x1, matrix products, per_device(): jnp.einsum('bmi,bmj->bij', widened * (inverse * inverse)[None, :, None],...  7.22 us
    dot_general x1, matrix products, per_device(): jnp.einsum('bmi,bmj->bij', widened * inverse[None, :, None], widened, pre...  7.04 us
  transfers between devices with their start and end apart: 12, of which 7 were waited for; matrix products, arithmetic and copies ran while one was open for 0% of the time, Pallas kernels for 0%

commit v1 on v0

v1 whole, which is shorter than its diff:
```python
import functools

import jax
import jax.numpy as jnp
from jax import lax
from jax.experimental import pallas as pl
from jax.experimental.pallas import tpu as pltpu
from jax.sharding import PartitionSpec as P

REACH = 3
SPOTS = 2 * REACH + 1
GROUP = 4
PANEL = 8
MESH_ID = pl.DeviceIdType.MESH
HIGHEST = lax.Precision.HIGHEST


def dot(a, b, over_a=1, over_b=0, precision=None):
    return lax.dot_general(
        a,
        b,
        (((over_a,), (over_b,)), ((), ())),
        precision=precision,
        preferred_element_type=jnp.float32,
    )


def in_two(x):
    high = x.astype(jnp.bfloat16)
    low = (x - high.astype(jnp.float32)).astype(jnp.bfloat16)
    return high, low


def project_kernel(
    size_ref, spot_ref, modes_ref, eig_ref, offset_ref, coupling_ref,
    projected_ref, stiff_ref, mass_ref, window_ref, inverse_ref,
):
    step = pl.program_id(0)
    half = modes_ref.shape[0] // 2
    width = coupling_ref.shape[2]
    depth = coupling_ref.shape[1]
    count = modes_ref.shape[1]
    size = size_ref[0]

    @pl.when(step == 0)
    def _():
        spots = lax.broadcasted_iota(jnp.int32, (half, count), 0)
        window = jnp.where(
            spots + half < size,
            modes_ref[half:, :].astype(jnp.float32),
            modes_ref[:half, :].astype(jnp.float32),
        )
        window_ref[...] = jnp.transpose(window).astype(jnp.bfloat16)
        inverse_ref[...] = jnp.transpose(
            jnp.broadcast_to(1.0 / eig_ref[...], (width, count))
        )
        stiff_ref[...] = jnp.zeros_like(stiff_ref)
        mass_ref[...] = jnp.zeros_like(mass_ref)

    inverse = inverse_ref[...]
    for pair in range(GROUP // 2):
        hot = []
        for block in (2 * pair, 2 * pair + 1):
            row = size - 1 - offset_ref[pl.ds(step * GROUP + block, 1), :]
            row = jnp.where(row >= half, row - half, row)
            spots = lax.broadcasted_iota(jnp.int32, (half, depth), 0)
            hot.append(jnp.where(spots == row, 1.0, 0.0).astype(jnp.bfloat16))
        picked = dot(window_ref[...], jnp.concatenate(hot, axis=1)).astype(jnp.bfloat16)
        for place in range(2):
            block = 2 * pair + place
            projected = dot(
                picked[:, place * depth:(place + 1) * depth], coupling_ref[block]
            ).astype(jnp.bfloat16)
            projected_ref[block] = projected
            once = projected.astype(jnp.float32) * inverse
            twice = once * inverse
            once_high, once_low = in_two(once)
            twice_high, twice_low = in_two(twice)
            turned = jnp.transpose(projected)
            terms = dot(turned, jnp.concatenate([once_high, twice_high], axis=1)) + dot(
                turned, jnp.concatenate([once_low, twice_low], axis=1)
            )
            spot = spot_ref[step * GROUP + block]
            stiff_ref[spot] += terms[:, :width]
            mass_ref[spot] += terms[:, width:]


def factor_rows(work_ref, rows_ref):
    width = work_ref.shape[0]

    def panel(at, carry):
        base = pl.multiple_of(at * PANEL, PANEL)
        block = work_ref[pl.ds(base, PANEL), :]
        ahead = pltpu.roll(block[:, :width], width - base, 1)
        entry = {}
        for i in range(PANEL):
            for j in range(i + 1):
                entry[i, j] = jnp.broadcast_to(ahead[j:j + 1, i:i + 1], (1, width))
        rows = [[block[i:i + 1, :width], block[i:i + 1, width:]] for i in range(PANEL)]
        for k in range(PANEL):
            pivot = entry[k, k]
            root = lax.rsqrt(pivot)
            root = root * (1.5 - 0.5 * pivot * root * root)
            for i in range(k + 1, PANEL):
                entry[i, k] = entry[i, k] * root
            rows[k] = [x * root for x in rows[k]]
            for i in range(k + 1, PANEL):
                for j in range(k + 1, i + 1):
                    entry[i, j] = entry[i, j] - entry[i, k] * entry[j, k]
                rows[i] = [x - entry[i, k] * y for x, y in zip(rows[i], rows[k])]
        done = jnp.concatenate(
            [jnp.concatenate([x[0] for x in rows], axis=0), jnp.concatenate([x[1] for x in rows], axis=0)],
            axis=1,
        )
        rows_ref[pl.ds(base, PANEL), :] = done
        work_ref[...] = work_ref[...] - dot(jnp.transpose(done[:, :width]), done, precision=HIGHEST)
        return carry

    lax.fori_loop(0, width // PANEL, panel, 0)


def exchange_kernel(
    stiff_ref, mass_ref, iface_ref, lumped_ref, reduced_ref, factor_ref, near_ref,
    stiff_in, mass_in, near_in, own_ref, work_ref, rows_ref, send_sem, recv_sem,
):
    length = lax.axis_size("sub")
    me = lax.axis_index("sub")
    width = lumped_ref.shape[1]
    others = [d for d in (-3, 3, -2, 2, -1, 1)]

    def device(by):
        return lax.rem(me + by + length, length)

    barrier = pltpu.get_barrier_semaphore()
    for d in others:
        pl.semaphore_signal(barrier, inc=1, device_id={"sub": device(d)}, device_id_type=MESH_ID)
    pl.semaphore_wait(barrier, len(others))

    def send(kind, source, landing, by, slot):
        copy = pltpu.make_async_remote_copy(
            src_ref=source,
            dst_ref=landing.at[slot],
            send_sem=send_sem.at[kind, slot],
            recv_sem=recv_sem.at[kind, slot],
            device_id={"sub": device(by)},
            device_id_type=MESH_ID,
        )
        copy.start()
        return copy

    mass_copies = [send(0, mass_ref.at[d + REACH], mass_in, d, d + REACH) for d in others]
    stiff_copies = [send(1, stiff_ref.at[d + REACH], stiff_in, d, d + REACH) for d in others]
    across = lax.broadcasted_iota(jnp.int32, (width, width), 0)
    along = lax.broadcasted_iota(jnp.int32, (width, width), 1)
    for copy in mass_copies:
        copy.wait_recv()
    mass = mass_ref[REACH]
    for d in others:
        mass = mass + mass_in[d + REACH]
    mass = mass + jnp.where(across == along, lumped_ref[...], 0.0)
    work_ref[:, :width] = mass
    work_ref[:, width:] = jnp.where(across == along, 1.0, 0.0)
    factor_rows(work_ref, rows_ref)
    own_ref[...] = jnp.transpose(jnp.where(across >= along, rows_ref[:, width:], 0.0))
    factor_ref[...] = jnp.transpose(jnp.where(across <= along, rows_ref[:, :width], 0.0))
    near_copies = [send(2, own_ref, near_in, -d, d + REACH) for d in others]
    for copy in stiff_copies:
        copy.wait_recv()
    stiff = stiff_ref[REACH]
    for d in others:
        stiff = stiff + stiff_in[d + REACH]
    reduced_ref[...] = iface_ref[0] - stiff
    for copy in mass_copies + stiff_copies:
        copy.wait_send()

    def place(slot, x):
        high, low = in_two(x)
        near_ref[slot, :width, :] = high
        near_ref[slot, width:, :] = low

    place(REACH, own_ref[...])
    for copy in near_copies:
        copy.wait()
    for d in others:
        place(d + REACH, near_in[d + REACH])


def couple_kernel(
    spot_ref, projected_ref, near_ref, reduced_in, factor_in, coupled_ref, reduced_ref, factor_ref
):
    step = pl.program_id(0)

    @pl.when(step == 0)
    def _():
        reduced_ref[0] = reduced_in[...]
        factor_ref[0] = factor_in[...]

    for block in range(GROUP):
        x = projected_ref[block]
        coupled_ref[block] = dot(
            jnp.concatenate([x, x], axis=1), near_ref[spot_ref[step * GROUP + block]]
        ).astype(jnp.bfloat16)


def per_device(
    modes, eigenvalues, sub_size, row_offset, stiff_coupling, iface_offset, stiff_iface, lumped_mass
):
    blocks, depth, width = stiff_coupling.shape
    most, count = modes.shape
    f32, bf16 = jnp.float32, jnp.bfloat16
    full = lambda *shape: pl.BlockSpec(shape, lambda i, *_: (0,) * len(shape))
    projected, stiff, mass = pl.pallas_call(
        project_kernel,
        grid_spec=pltpu.PrefetchScalarGridSpec(
            num_scalar_prefetch=2,
            grid=(blocks // GROUP,),
            in_specs=[
                full(most, count),
                full(1, count),
                full(blocks, depth),
                pl.BlockSpec((GROUP, depth, width), lambda i, *_: (i, 0, 0)),
            ],
            out_specs=[
                pl.BlockSpec((GROUP, count, width), lambda i, *_: (i, 0, 0)),
                full(SPOTS, width, width),
                full(SPOTS, width, width),
            ],
            scratch_shapes=[
                pltpu.VMEM((count, most // 2), bf16),
                pltpu.VMEM((count, width), f32),
            ],
        ),
        out_shape=[
            jax.ShapeDtypeStruct((blocks, count, width), bf16),
            jax.ShapeDtypeStruct((SPOTS, width, width), f32),
            jax.ShapeDtypeStruct((SPOTS, width, width), f32),
        ],
        compiler_params=pltpu.CompilerParams(dimension_semantics=("arbitrary",)),
        name="project",
    )(sub_size, iface_offset, modes, eigenvalues, row_offset, stiff_coupling)

    vmem = pl.BlockSpec(memory_space=pltpu.VMEM)
    reduced, factor, near = pl.pallas_call(
        exchange_kernel,
        in_specs=[vmem] * 4,
        out_specs=[vmem] * 3,
        out_shape=[
            jax.ShapeDtypeStruct((width, width), f32),
            jax.ShapeDtypeStruct((width, width), f32),
            jax.ShapeDtypeStruct((SPOTS, 2 * width, width), bf16),
        ],
        scratch_shapes=[
            pltpu.VMEM((SPOTS, width, width), f32),
            pltpu.VMEM((SPOTS, width, width), f32),
            pltpu.VMEM((SPOTS, width, width), f32),
            pltpu.VMEM((width, width), f32),
            pltpu.VMEM((width, 2 * width), f32),
            pltpu.VMEM((width, 2 * width), f32),
            pltpu.SemaphoreType.DMA((3, SPOTS)),
            pltpu.SemaphoreType.DMA((3, SPOTS)),
        ],
        compiler_params=pltpu.CompilerParams(collective_id=0, has_side_effects=True),
        name="exchange",
    )(stiff, mass, stiff_iface, lumped_mass)

    coupled, reduced, factor = pl.pallas_call(
        couple_kernel,
        grid_spec=pltpu.PrefetchScalarGridSpec(
            num_scalar_prefetch=1,
            grid=(blocks // GROUP,),
            in_specs=[
                pl.BlockSpec((GROUP, count, width), lambda i, *_: (i, 0, 0)),
                full(SPOTS, 2 * width, width),
                full(width, width),
                full(width, width),
            ],
            out_specs=[
                pl.BlockSpec((GROUP, count, width), lambda i, *_: (i, 0, 0)),
                full(1, width, width),
                full(1, width, width),
            ],
        ),
        out_shape=[
            jax.ShapeDtypeStruct((blocks, count, width), bf16),
            jax.ShapeDtypeStruct((1, width, width), f32),
            jax.ShapeDtypeStruct((1, width, width), f32),
        ],
        compiler_params=pltpu.CompilerParams(dimension_semantics=("arbitrary",)),
        name="couple",
    )(iface_offset, projected, near, reduced, factor)
    return reduced, factor, coupled


def solution(mesh):
    placed = (
        P(("groups", "sub"), None),
        P(("groups", "sub"), None),
        P(("groups", "sub")),
        P(("groups", "sub"), None),
        P(("groups", "sub"), None, None),
        P(("groups", "sub")),
        P(("groups", "sub"), None, None),
        P(("groups", "sub"), None),
    )
    return jax.shard_map(
        per_device,
        mesh=mesh,
        in_specs=placed,
        out_specs=(
            P(("groups", "sub"), None, None),
            P(("groups", "sub"), None, None),
            P(("groups", "sub"), None, None),
        ),
        check_vma=False,
    )
```

time: 114 us -> 68.3 us (0.60)
  Pallas kernels: 0 us -> 66.6 us
  matrix products: 29.8 us -> 0 us
  local copies, waits for them, and re-layouts: 26.8 us -> 0 us
  other arithmetic: 25.9 us -> 0 us
  starting transfers between devices: 20.1 us -> 0 us
  waiting for transfers between devices: 9.81 us -> 0 us
    pallas_call x0 -> x3, Pallas kernels: none -> 66.6 us  [the longest x1 32.6 us: per_device(): pl.pallas_call(exchange_kernel, in_specs=[vmem] * 4, out_specs=[vmem] * 3...]
    dot_general x5 -> x0, matrix products: 29.6 us -> none  [the longest x1 7.97 us: per_device(): jnp.einsum('bmi,bji->bmj', widened, chosen, precision=lax.Precision.HIGHEST)]
    gather x3 -> x0, local copies, waits for them, and re-layouts: 25.9 us -> none  [the longest x2 23.9 us: per_device(): picked = jnp.take(modes, picked_rows, axis=0)]
    another operation x6 -> x0, other arithmetic: 23.8 us -> none  [the longest x3 12.4 us: per_device(): factor = jnp.linalg.cholesky(mass_matrix)]
    ppermute x12 -> x0, starting transfers between devices: 20.1 us -> none  [passed_along(): lax.ppermute(x, axis, [(i, (i + by) % length) for i in range(length)])]
    ppermute x12 -> x0, waiting for transfers between devices: 9.81 us -> none  [passed_along(): lax.ppermute(x, axis, [(i, (i + by) % length) for i in range(length)])]
  transfers between devices with their start and end apart: 12 -> 0, of which waited for: 7 -> 0; matrix products, arithmetic and copies ran while one was open for 0% -> 0% of each run, Pallas kernels for 0% -> 0%
where the time goes in v1:
time: 68.3 us; the launch traced here: 67.9 us
  Pallas kernels  66.6 us (98%)
  between operations  1.29 us (2%)
    pallas_call x1, Pallas kernels, per_device(): pl.pallas_call(exchange_kernel, in_specs=[vmem] * 4, out_specs=[vmem] * 3...  32.6 us
    pallas_call x1, Pallas kernels, per_device(): pl.pallas_call(project_kernel, grid_spec=pltpu.PrefetchScalarGridSpec(num...  25.2 us
    pallas_call x1, Pallas kernels, per_device(): pl.pallas_call(couple_kernel, grid_spec=pltpu.PrefetchScalarGridSpec(num_...  8.87 us

profile of v1, /device:TPU:0, one launch (start us, length us, event | category | flops | bytes accessed | tf_op | source)
XLA Modules:
  0.0 67.9 jit_solution(11195529489241989904)
XLA Ops:
  1.3 25.2 %project.1 = (bf16[32,512,128]{2,1,0:T(8,128)(2,1)}, f32[7,128,128]{2,1,0:T(8,128)}, f32[7,128,128]{2,1,0:T(8,128)}) custom-call(s32[1]{0:T(128)S(6)} %copy.11.size_ref, s32[32]{0:T(128)} %spot_ref.3, bf16[2048,512]{1,0:T(8,128)(2,1)} %modes_ref.1, f32[1,512]{1,0:T(1,128)} %eig_ref.1, s32[32,128]{1,0:T(8,128)} %offset_ref.1, bf16[32,128,128]{2,1,0:T(8,128)(2,1)} %coupling_ref.1), custom_call_target="tpu_custom_call" | custom-call | tf_op jit(solution)/shard_map/project/pallas_call | solution.py:212
  26.5 32.6 %exchange.1 = (f32[128,128]{1,0:T(8,128)}, f32[128,128]{1,0:T(8,128)}, bf16[7,256,128]{2,1,0:T(8,128)(2,1)}) custom-call(f32[7,128,128]{2,1,0:T(8,128)} %get-tuple-element.13.stiff_ref, f32[7,128,128]{2,1,0:T(8,128)} %get-tuple-element.14.mass_ref, f32[1,128,128]{2,1,0:T(8,128)} %iface_ref.1, f32[1,128]{1,0:T(1,128)} %lumped_ref.1), custom_call_target="tpu_custom_call" | custom-call | tf_op jit(solution)/shard_map/exchange/pallas_call | solution.py:243
  59.0 8.9 %couple.1 = (bf16[32,512,128]{2,1,0:T(8,128)(2,1)}, f32[1,128,128]{2,1,0:T(8,128)}, f32[1,128,128]{2,1,0:T(8,128)}) custom-call(s32[32]{0:T(128)} %spot_ref.3, bf16[32,512,128]{2,1,0:T(8,128)(2,1)} %get-tuple-element.12.projected_ref, bf16[7,256,128]{2,1,0:T(8,128)(2,1)} %get-tuple-element.15.near_ref, f32[128,128]{1,0:T(8,128)} %get-tuple-element.16.reduced_in, ...), custom_call_target="tpu_custom_call" | custom-call | tf_op jit(solution)/shard_map/couple/pallas_call | solution.py:266

commit v2 on v1

v2 whole, which is shorter than its diff:
```python
import functools

import jax
import jax.numpy as jnp
from jax import lax
from jax.experimental import pallas as pl
from jax.experimental.pallas import tpu as pltpu
from jax.sharding import PartitionSpec as P

REACH = 3
SPOTS = 2 * REACH + 1
GROUP = 4
PANEL = 8
PIECES = 4
MESH_ID = pl.DeviceIdType.MESH
HIGHEST = lax.Precision.HIGHEST


def dot(a, b, over_a=1, over_b=0, precision=None):
    return lax.dot_general(
        a,
        b,
        (((over_a,), (over_b,)), ((), ())),
        precision=precision,
        preferred_element_type=jnp.float32,
    )


def in_two(x):
    high = x.astype(jnp.bfloat16)
    low = (x - high.astype(jnp.float32)).astype(jnp.bfloat16)
    return high, low


def project_kernel(
    size_ref, spot_ref, offset_ref, modes_ref, eig_ref, coupling_ref,
    projected_ref, stiff_ref, packed_ref, mass_ref, rows_ref, inverse_ref, first_ref, start_ref, sem, *picked_refs,
):
    step = pl.program_id(0)
    depth, width = coupling_ref.shape[1:]
    most, count = modes_ref.shape
    parts = count // width
    blocks = offset_ref.shape[0]

    def gather(at, into, low, high):
        for r in range(low, high):
            into[pl.ds(r * parts, parts), :] = rows_ref[pl.ds(start_ref[at, r], parts), :]

    @pl.when(step == 0)
    def _():
        first_ref[...] = (size_ref[0] - 1 - offset_ref[...]) * parts
        for chunk in range(parts):
            rows_ref[pl.ds(chunk, most, stride=parts), :] = modes_ref[
                :, chunk * width:(chunk + 1) * width
            ].astype(jnp.float32)
            if chunk == 0:
                starts = pltpu.make_async_copy(first_ref, start_ref, sem)
                starts.start()
        inverse_ref[...] = 1.0 / jnp.broadcast_to(eig_ref[...], inverse_ref.shape)
        stiff_ref[...] = jnp.zeros_like(stiff_ref)
        mass_ref[...] = jnp.zeros_like(mass_ref)
        starts.wait()
        gather(0, picked_refs[0], 0, depth)

    for block in range(GROUP):
        at = step * GROUP + block
        following = jnp.minimum(at + 1, blocks - 1)
        into = picked_refs[(block + 1) % GROUP]
        source = picked_refs[block]
        picked = jnp.concatenate(
            [source[pl.ds(chunk, depth, stride=parts), :].astype(jnp.bfloat16) for chunk in range(parts)],
            axis=1,
        )
        gather(following, into, 0, depth // 2)
        turned = dot(jnp.transpose(coupling_ref[block]), picked).astype(jnp.bfloat16)
        projected_ref[block] = jnp.transpose(turned)
        gather(following, into, depth // 2, depth)
        inverse = inverse_ref[...]
        wide = turned.astype(jnp.float32)
        once = wide * inverse
        twice = once * inverse
        once_high, once_low = in_two(once)
        twice_high, twice_low = in_two(twice)
        high = jnp.concatenate([once_high, twice_high], axis=0)
        low = jnp.concatenate([once_low, twice_low], axis=0)
        terms = dot(turned, high, 1, 1) + dot(turned, low, 1, 1)
        spot = spot_ref[at]
        stiff_ref[spot] += terms[:, :width]
        mass_ref[spot] += terms[:, width:]

    @pl.when(step == pl.num_programs(0) - 1)
    def _():
        half = width // 2
        across = lax.broadcasted_iota(jnp.int32, (half, width), 0)
        along = lax.broadcasted_iota(jnp.int32, (half, width), 1)
        for slot in range(SPOTS):
            moved = pltpu.roll(mass_ref[slot, half:, :], half, 1)
            packed_ref[slot, :half, :] = jnp.where(along < across, moved, mass_ref[slot, :half, :])
            diagonal = jnp.sum(jnp.where(along == across, moved, 0.0), axis=0, keepdims=True)
            packed_ref[slot, half:, :] = jnp.broadcast_to(diagonal, (PANEL, width))


def factor_rows(work_ref, rows_ref, first, last):
    width = work_ref.shape[0]

    def panel(at, carry):
        base = pl.multiple_of(at * PANEL, PANEL)
        block = work_ref[pl.ds(base, PANEL), :]
        ahead = pltpu.roll(block[:, :width], width - base, 1)
        entry = {}
        for i in range(PANEL):
            for j in range(i + 1):
                entry[i, j] = jnp.broadcast_to(ahead[j:j + 1, i:i + 1], (1, width))
        rows = [[block[i:i + 1, :width], block[i:i + 1, width:]] for i in range(PANEL)]
        for k in range(PANEL):
            pivot = entry[k, k]
            root = lax.rsqrt(pivot)
            root = root * (1.5 - 0.5 * pivot * root * root)
            for i in range(k + 1, PANEL):
                entry[i, k] = entry[i, k] * root
            rows[k] = [x * root for x in rows[k]]
            for i in range(k + 1, PANEL):
                for j in range(k + 1, i + 1):
                    entry[i, j] = entry[i, j] - entry[i, k] * entry[j, k]
                rows[i] = [x - entry[i, k] * y for x, y in zip(rows[i], rows[k])]
        done = jnp.concatenate(
            [jnp.concatenate([x[0] for x in rows], axis=0), jnp.concatenate([x[1] for x in rows], axis=0)],
            axis=1,
        )
        rows_ref[pl.ds(base, PANEL), :] = done
        work_ref[...] = work_ref[...] - dot(jnp.transpose(done[:, :width]), done, precision=HIGHEST)
        return carry

    lax.fori_loop(first // PANEL, last // PANEL, panel, 0)


def exchange_kernel(
    stiff_ref, mass_ref, iface_ref, lumped_ref, reduced_ref, factor_ref, near_ref,
    stiff_in, mass_in, near_in, own_ref, work_ref, rows_ref, send_sem, recv_sem, local_sem,
):
    length = lax.axis_size("sub")
    me = lax.axis_index("sub")
    width = lumped_ref.shape[1]
    half = width // 2
    others = (-3, 3, -2, 2, -1, 1)

    def device(by):
        return lax.rem(me + by + length, length)

    own_mass = pltpu.make_async_copy(mass_ref.at[REACH], mass_in.at[REACH], local_sem.at[0])
    own_stiff = pltpu.make_async_copy(stiff_ref.at[REACH], stiff_in.at[REACH], local_sem.at[1])
    own_mass.start()
    own_stiff.start()
    barrier = pltpu.get_barrier_semaphore()
    for d in others:
        pl.semaphore_signal(barrier, inc=1, device_id={"sub": device(d)}, device_id_type=MESH_ID)
    pl.semaphore_wait(barrier, len(others))

    def send(kind, source, landing, by, slot):
        copy = pltpu.make_async_remote_copy(
            src_ref=source,
            dst_ref=landing,
            send_sem=send_sem.at[kind, slot],
            recv_sem=recv_sem.at[kind, slot],
            device_id={"sub": device(by)},
            device_id_type=MESH_ID,
        )
        copy.start()
        return copy

    mass_copies = [
        send(0, mass_ref.at[d + REACH], mass_in.at[d + REACH], d, d + REACH) for d in others
    ]
    across = lax.broadcasted_iota(jnp.int32, (width, width), 0)
    along = lax.broadcasted_iota(jnp.int32, (width, width), 1)
    own_mass.wait()
    for copy in mass_copies:
        copy.wait_recv()
    stiff_copies = [
        send(1, stiff_ref.at[d + REACH], stiff_in.at[d + REACH], d, d + REACH) for d in others
    ]
    packed = mass_in[REACH]
    for d in others:
        packed = packed + mass_in[d + REACH]
    top = packed[:half]
    low = jnp.concatenate([jnp.zeros_like(top), pltpu.roll(top, half, 1)], axis=0)
    low = jnp.transpose(jnp.where((across >= half) & (along >= half) & (along < across), low, 0.0))
    diagonal = pltpu.roll(packed[half:half + 1], half, 1)
    bottom = jnp.where(across[half:] == along[half:], diagonal, low[half:])
    mass = jnp.concatenate([top, bottom], axis=0)
    work_ref[:, :width] = jnp.where(across == along, mass + lumped_ref[...], mass)
    work_ref[:, width:] = jnp.where(across == along, 1.0, 0.0)
    near_copies = []
    rows = width // PIECES
    for piece in range(PIECES):
        part = pl.ds(piece * rows, rows)
        factor_rows(work_ref, rows_ref, piece * rows, (piece + 1) * rows)
        begun = slice(piece * rows, (piece + 1) * rows)
        own_ref[part, :] = jnp.where(across[begun] >= along[begun], rows_ref[part, width:], 0.0)
        near_copies += [
            send(2 + piece, own_ref.at[part], near_in.at[d + REACH, part], -d, d + REACH) for d in others
        ]
    factor_ref[...] = jnp.transpose(jnp.where(across <= along, rows_ref[:, :width], 0.0))
    own_stiff.wait()
    for copy in stiff_copies:
        copy.wait_recv()
    stiff = stiff_in[REACH]
    for d in others:
        stiff = stiff + stiff_in[d + REACH]
    reduced_ref[...] = iface_ref[0] - stiff
    for copy in mass_copies + stiff_copies:
        copy.wait_send()

    def place(slot, x):
        high, low = in_two(x)
        near_ref[slot, :, :width] = high
        near_ref[slot, :, width:] = low

    place(REACH, own_ref[...])
    for copy in near_copies:
        copy.wait()
    for d in others:
        place(d + REACH, near_in[d + REACH])


def couple_kernel(
    spot_ref, projected_ref, near_ref, reduced_in, factor_in, coupled_ref, reduced_ref, factor_ref
):
    step = pl.program_id(0)

    @pl.when(step == 0)
    def _():
        reduced_ref[0] = reduced_in[...]
        factor_ref[0] = factor_in[...]

    for block in range(GROUP):
        x = projected_ref[block]
        coupled_ref[block] = dot(
            jnp.concatenate([x, x], axis=1), near_ref[spot_ref[step * GROUP + block]], 1, 1
        ).astype(jnp.bfloat16)


def per_device(
    modes, eigenvalues, sub_size, row_offset, stiff_coupling, iface_offset, stiff_iface, lumped_mass
):
    blocks, depth, width = stiff_coupling.shape
    most, count = modes.shape
    f32, bf16 = jnp.float32, jnp.bfloat16
    full = lambda *shape: pl.BlockSpec(shape, lambda i, *_: (0,) * len(shape))
    projected, stiff, mass = pl.pallas_call(
        project_kernel,
        grid_spec=pltpu.PrefetchScalarGridSpec(
            num_scalar_prefetch=2,
            grid=(blocks // GROUP,),
            in_specs=[
                full(blocks, depth),
                full(most, count),
                full(1, count),
                pl.BlockSpec((GROUP, depth, width), lambda i, *_: (i, 0, 0)),
            ],
            out_specs=[
                pl.BlockSpec((GROUP, count, width), lambda i, *_: (i, 0, 0)),
                full(SPOTS, width, width),
                full(SPOTS, width // 2 + PANEL, width),
            ],
            scratch_shapes=[
                pltpu.VMEM((SPOTS, width, width), f32),
                pltpu.VMEM((most * count // width, width), f32),
                pltpu.VMEM((width, count), f32),
                pltpu.VMEM((blocks, depth), jnp.int32),
                pltpu.SMEM((blocks, depth), jnp.int32),
                pltpu.SemaphoreType.DMA,
            ]
            + [pltpu.VMEM((depth * count // width, width), f32)] * GROUP,
        ),
        out_shape=[
            jax.ShapeDtypeStruct((blocks, count, width), bf16),
            jax.ShapeDtypeStruct((SPOTS, width, width), f32),
            jax.ShapeDtypeStruct((SPOTS, width // 2 + PANEL, width), f32),
        ],
        compiler_params=pltpu.CompilerParams(dimension_semantics=("arbitrary",)),
        name="project",
    )(sub_size, iface_offset, row_offset, modes, eigenvalues, stiff_coupling)

    vmem = pl.BlockSpec(memory_space=pltpu.VMEM)
    reduced, factor, near = pl.pallas_call(
        exchange_kernel,
        in_specs=[pl.BlockSpec(memory_space=pl.ANY)] * 2 + [vmem] * 2,
        out_specs=[vmem] * 3,
        out_shape=[
            jax.ShapeDtypeStruct((width, width), f32),
            jax.ShapeDtypeStruct((width, width), f32),
            jax.ShapeDtypeStruct((SPOTS, width, 2 * width), bf16),
        ],
        scratch_shapes=[
            pltpu.VMEM((SPOTS, width, width), f32),
            pltpu.VMEM((SPOTS, width // 2 + PANEL, width), f32),
            pltpu.VMEM((SPOTS, width, width), f32),
            pltpu.VMEM((width, width), f32),
            pltpu.VMEM((width, 2 * width), f32),
            pltpu.VMEM((width, 2 * width), f32),
            pltpu.SemaphoreType.DMA((2 + PIECES, SPOTS)),
            pltpu.SemaphoreType.DMA((2 + PIECES, SPOTS)),
            pltpu.SemaphoreType.DMA((2,)),
        ],
        compiler_params=pltpu.CompilerParams(collective_id=0, has_side_effects=True),
        name="exchange",
    )(stiff, mass, stiff_iface, lumped_mass)

    coupled, reduced, factor = pl.pallas_call(
        couple_kernel,
        grid_spec=pltpu.PrefetchScalarGridSpec(
            num_scalar_prefetch=1,
            grid=(blocks // GROUP,),
            in_specs=[
                pl.BlockSpec((GROUP, count, width), lambda i, *_: (i, 0, 0)),
                full(SPOTS, width, 2 * width),
                full(width, width),
                full(width, width),
            ],
            out_specs=[
                pl.BlockSpec((GROUP, count, width), lambda i, *_: (i, 0, 0)),
                full(1, width, width),
                full(1, width, width),
            ],
        ),
        out_shape=[
            jax.ShapeDtypeStruct((blocks, count, width), bf16),
            jax.ShapeDtypeStruct((1, width, width), f32),
            jax.ShapeDtypeStruct((1, width, width), f32),
        ],
        compiler_params=pltpu.CompilerParams(dimension_semantics=("arbitrary",)),
        name="couple",
    )(iface_offset, projected, near, reduced, factor)
    return reduced, factor, coupled


def solution(mesh):
    placed = (
        P(("groups", "sub"), None),
        P(("groups", "sub"), None),
        P(("groups", "sub")),
        P(("groups", "sub"), None),
        P(("groups", "sub"), None, None),
        P(("groups", "sub")),
        P(("groups", "sub"), None, None),
        P(("groups", "sub"), None),
    )
    return jax.shard_map(
        per_device,
        mesh=mesh,
        in_specs=placed,
        out_specs=(
            P(("groups", "sub"), None, None),
            P(("groups", "sub"), None, None),
            P(("groups", "sub"), None, None),
        ),
        check_vma=False,
    )
```

time: 68.3 us -> 53.9 us (0.79)
  Pallas kernels: 66.6 us -> 52.2 us
    pallas_call x1, Pallas kernels: 25.2 us -> 15.7 us  [per_device(): pl.pallas_call(project_kernel, grid_spec=pltpu.PrefetchScalarGridSpec(num...]
    pallas_call x1, Pallas kernels: 32.6 us -> 27.7 us  [per_device(): pl.pallas_call(exchange_kernel, in_specs=[pl.BlockSpec(memory_space=pl.AN...]
where the time goes in v2:
time: 53.9 us; the launch traced here: 53.5 us
  Pallas kernels  52.2 us (97%)
  between operations  1.29 us (2%)
    pallas_call x1, Pallas kernels, per_device(): pl.pallas_call(exchange_kernel, in_specs=[pl.BlockSpec(memory_space=pl.AN...  27.7 us
    pallas_call x1, Pallas kernels, per_device(): pl.pallas_call(project_kernel, grid_spec=pltpu.PrefetchScalarGridSpec(num...  15.7 us
    pallas_call x1, Pallas kernels, per_device(): pl.pallas_call(couple_kernel, grid_spec=pltpu.PrefetchScalarGridSpec(num_...  8.86 us

profile of v2, /device:TPU:0, one launch (start us, length us, event | category | flops | bytes accessed | tf_op | source)
XLA Modules:
  0.0 53.5 jit_solution(3505086722901528361)
XLA Ops:
  1.3 15.7 %project.1 = (bf16[32,512,128]{2,1,0:T(8,128)(2,1)}, f32[7,128,128]{2,1,0:T(8,128)}, f32[7,72,128]{2,1,0:T(8,128)}) custom-call(s32[1]{0:T(128)S(6)} %copy.11.size_ref, s32[32]{0:T(128)} %spot_ref.3, s32[32,128]{1,0:T(8,128)} %offset_ref.1, bf16[2048,512]{1,0:T(8,128)(2,1)} %modes_ref.1, f32[1,512]{1,0:T(1,128)} %eig_ref.1, bf16[32,128,128]{2,1,0:T(8,128)(2,1)} %coupling_ref.1), custom_call_target="tpu_custom_call" | custom-call | tf_op jit(solution)/shard_map/project/pallas_call | solution.py:250
  16.9 27.7 %exchange.1 = (f32[128,128]{1,0:T(8,128)}, f32[128,128]{1,0:T(8,128)}, bf16[7,128,256]{2,1,0:T(8,128)(2,1)}) custom-call(f32[7,128,128]{2,1,0:T(8,128)} %get-tuple-element.13.stiff_ref, f32[7,72,128]{2,1,0:T(8,128)} %get-tuple-element.14.mass_ref, f32[1,128,128]{2,1,0:T(8,128)} %iface_ref.1, f32[1,128]{1,0:T(1,128)} %lumped_ref.1), custom_call_target="tpu_custom_call" | custom-call | tf_op jit(solution)/shard_map/exchange/pallas_call | solution.py:286
  44.7 8.9 %couple.1 = (bf16[32,512,128]{2,1,0:T(8,128)(2,1)}, f32[1,128,128]{2,1,0:T(8,128)}, f32[1,128,128]{2,1,0:T(8,128)}) custom-call(s32[32]{0:T(128)} %spot_ref.3, bf16[32,512,128]{2,1,0:T(8,128)(2,1)} %get-tuple-element.12.projected_ref, bf16[7,128,256]{2,1,0:T(8,128)(2,1)} %get-tuple-element.15.near_ref, f32[128,128]{1,0:T(8,128)} %get-tuple-element.16.reduced_in, ...), custom_call_target="tpu_custom_call" | custom-call | tf_op jit(solution)/shard_map/couple/pallas_call | solution.py:310

commit v3 on v2

--- a/solution.py
+++ b/solution.py
@@ -13,15 +13,14 @@
 PANEL = 8
 PIECES = 4
 MESH_ID = pl.DeviceIdType.MESH
-HIGHEST = lax.Precision.HIGHEST
-
-
-def dot(a, b, over_a=1, over_b=0, precision=None):
+MIB = 1 << 20
+
+
+def dot(a, b, over_a=1, over_b=0):
     return lax.dot_general(
         a,
         b,
         (((over_a,), (over_b,)), ((), ())),
-        precision=precision,
         preferred_element_type=jnp.float32,
     )
 
@@ -30,6 +29,12 @@
     high = x.astype(jnp.bfloat16)
     low = (x - high.astype(jnp.float32)).astype(jnp.bfloat16)
     return high, low
+
+
+def in_three(x):
+    high = x.astype(jnp.bfloat16).astype(jnp.float32)
+    middle = (x - high).astype(jnp.bfloat16).astype(jnp.float32)
+    return high, middle, x - high - middle
 
 
 def project_kernel(
@@ -128,7 +133,11 @@
             axis=1,
         )
         rows_ref[pl.ds(base, PANEL), :] = done
-        work_ref[...] = work_ref[...] - dot(jnp.transpose(done[:, :width]), done, precision=HIGHEST)
+        high, middle, low = in_three(done)
+        left = jnp.concatenate([x[:, :width] for x in (high, high, middle, middle, high, low)], axis=0)
+        right = jnp.concatenate([high, middle, high, middle, low, high], axis=0)
+        left = jnp.transpose(left).astype(jnp.bfloat16)
+        work_ref[...] = work_ref[...] - dot(left, right.astype(jnp.bfloat16))
         return carry
 
     lax.fori_loop(first // PANEL, last // PANEL, panel, 0)
@@ -278,7 +287,9 @@
             jax.ShapeDtypeStruct((SPOTS, width, width), f32),
             jax.ShapeDtypeStruct((SPOTS, width // 2 + PANEL, width), f32),
         ],
-        compiler_params=pltpu.CompilerParams(dimension_semantics=("arbitrary",)),
+        compiler_params=pltpu.CompilerParams(
+            dimension_semantics=("arbitrary",), vmem_limit_bytes=20 * MIB
+        ),
         name="project",
     )(sub_size, iface_offset, row_offset, modes, eigenvalues, stiff_coupling)
 
@@ -303,7 +314,9 @@
             pltpu.SemaphoreType.DMA((2 + PIECES, SPOTS)),
             pltpu.SemaphoreType.DMA((2,)),
         ],
-        compiler_params=pltpu.CompilerParams(collective_id=0, has_side_effects=True),
+        compiler_params=pltpu.CompilerParams(
+            collective_id=0, has_side_effects=True, vmem_limit_bytes=8 * MIB
+        ),
         name="exchange",
     )(stiff, mass, stiff_iface, lumped_mass)
 
@@ -329,7 +342,9 @@
             jax.ShapeDtypeStruct((1, width, width), f32),
             jax.ShapeDtypeStruct((1, width, width), f32),
         ],
-        compiler_params=pltpu.CompilerParams(dimension_semantics=("arbitrary",)),
+        compiler_params=pltpu.CompilerParams(
+            dimension_semantics=("arbitrary",), vmem_limit_bytes=12 * MIB
+        ),
         name="couple",
     )(iface_offset, projected, near, reduced, factor)
     return reduced, factor, coupled

time: 53.9 us -> 51.1 us (0.948)
  Pallas kernels: 52.2 us -> 43.1 us
  local copies, waits for them, and re-layouts: 0 us -> 6.35 us
    unnamed x0 -> x14, local copies, waits for them, and re-layouts: none -> 6.35 us
    pallas_call x1, Pallas kernels: 27.7 us -> 24.6 us  [per_device(): pl.pallas_call(exchange_kernel, in_specs=[pl.BlockSpec(memory_space=pl.AN...]
    pallas_call x1, Pallas kernels: 15.7 us -> 12.6 us  [per_device(): pl.pallas_call(project_kernel, grid_spec=pltpu.PrefetchScalarGridSpec(num...]
    pallas_call x1, Pallas kernels: 8.86 us -> 5.95 us  [per_device(): pl.pallas_call(couple_kernel, grid_spec=pltpu.PrefetchScalarGridSpec(num_...]
where the time goes in v3:
time: 51.1 us; the launch traced here: 50.8 us
  Pallas kernels  43.1 us (84%)
  local copies, waits for them, and re-layouts  6.35 us (12%)
  between operations  1.31 us (3%)
    pallas_call x1, Pallas kernels, per_device(): pl.pallas_call(exchange_kernel, in_specs=[pl.BlockSpec(memory_space=pl.AN...  24.6 us
    pallas_call x1, Pallas kernels, per_device(): pl.pallas_call(project_kernel, grid_spec=pltpu.PrefetchScalarGridSpec(num...  12.6 us
    unnamed x14, local copies, waits for them, and re-layouts  6.35 us
    pallas_call x1, Pallas kernels, per_device(): pl.pallas_call(couple_kernel, grid_spec=pltpu.PrefetchScalarGridSpec(num_...  5.95 us

profile of v3, /device:TPU:0, one launch (start us, length us, event | category | flops | bytes accessed | tf_op | source)
XLA Modules:
  0.0 50.8 jit_solution(11707427338253360747)
XLA Ops:
  1.3 0.0 copy-start
  1.3 1.6 %copy-done = bf16[2048,512]{1,0:T(8,128)(2,1)S(1)} copy-done((bf16[2048,512]{1,0:T(8,128)(2,1)S(1)}, bf16[2048,512]{1,0:T(8,128)(2,1)}, u32[]{:S(2)}) %copy-start) | copy-done | bytes 2097176
  2.9 0.0 copy-start.1
  2.9 1.2 %copy-done.1 = bf16[32,128,128]{2,1,0:T(8,128)(2,1)S(1)} copy-done((bf16[32,128,128]{2,1,0:T(8,128)(2,1)S(1)}, bf16[32,128,128]{2,1,0:T(8,128)(2,1)}, u32[]{:S(2)}) %copy-start.1) | copy-done | bytes 1048600
  4.1 0.0 copy-start.3
  4.1 0.7 %copy-done.3 = s32[32,128]{1,0:T(8,128)S(1)} copy-done((s32[32,128]{1,0:T(8,128)S(1)}, s32[32,128]{1,0:T(8,128)}, u32[]{:S(2)}) %copy-start.3) | copy-done | bytes 16408
  4.8 0.0 copy-start.4
  4.8 0.7 %copy-done.4 = f32[1,512]{1,0:T(1,128)S(1)} copy-done((f32[1,512]{1,0:T(1,128)S(1)}, f32[1,512]{1,0:T(1,128)}, u32[]{:S(2)}) %copy-start.4) | copy-done | bytes 2072
  5.5 0.0 copy-start.5
  5.5 0.7 %copy-done.5 = s32[32]{0:T(128)S(1)} copy-done((s32[32]{0:T(128)S(1)}, s32[32]{0:T(128)}, u32[]{:S(2)}) %copy-start.5) | copy-done | bytes 152
  6.2 12.6 %project.1 = (bf16[32,512,128]{2,1,0:T(8,128)(2,1)S(1)}, f32[7,128,128]{2,1,0:T(8,128)S(1)}, f32[7,72,128]{2,1,0:T(8,128)S(1)}) custom-call(s32[1]{0:T(128)S(6)} %copy.11.size_ref, s32[32]{0:T(128)S(1)} %copy-done.5, s32[32,128]{1,0:T(8,128)S(1)} %copy-done.3, bf16[2048,512]{1,0:T(8,128)(2,1)S(1)} %copy-done, f32[1,512]{1,0:T(1,128)S(1)} %copy-done.4, ...), custom_call_target="tpu_custom_call" | custom-call | tf_op jit(solution)/shard_map/project/pallas_call | solution.py:259
  18.8 0.0 copy-start.2
  18.8 0.8 %copy-done.2 = f32[1,128,128]{2,1,0:T(8,128)S(1)} copy-done((f32[1,128,128]{2,1,0:T(8,128)S(1)}, f32[1,128,128]{2,1,0:T(8,128)}, u32[]{:S(2)}) %copy-start.2) | copy-done | bytes 65560
  19.6 0.0 copy-start.6
  19.6 0.7 %copy-done.6 = f32[1,128]{1,0:T(1,128)S(1)} copy-done((f32[1,128]{1,0:T(1,128)S(1)}, f32[1,128]{1,0:T(1,128)}, u32[]{:S(2)}) %copy-start.6) | copy-done | bytes 536
  20.3 24.6 %exchange.1 = (f32[128,128]{1,0:T(8,128)S(1)}, f32[128,128]{1,0:T(8,128)S(1)}, bf16[7,128,256]{2,1,0:T(8,128)(2,1)S(1)}) custom-call(f32[7,128,128]{2,1,0:T(8,128)S(1)} %get-tuple-element.13.stiff_ref, f32[7,72,128]{2,1,0:T(8,128)S(1)} %get-tuple-element.14.mass_ref, f32[1,128,128]{2,1,0:T(8,128)S(1)} %copy-done.2, f32[1,128]{1,0:T(1,128)S(1)} %copy-done.6), custom_call_target="tpu_custom_call" | custom-call | tf_op jit(solution)/shard_map/exchange/pallas_call | solution.py:297
  44.8 6.0 %couple.1 = (bf16[32,512,128]{2,1,0:T(8,128)(2,1)}, f32[1,128,128]{2,1,0:T(8,128)}, f32[1,128,128]{2,1,0:T(8,128)}) custom-call(s32[32]{0:T(128)S(1)} %copy-done.5, bf16[32,512,128]{2,1,0:T(8,128)(2,1)S(1)} %get-tuple-element.12.projected_ref, bf16[7,128,256]{2,1,0:T(8,128)(2,1)S(1)} %get-tuple-element.15.near_ref, ...), custom_call_target="tpu_custom_call" | custom-call | tf_op jit(solution)/shard_map/couple/pallas_call | solution.py:323
Async XLA Ops:
  1.3 1.6 %copy-start = (bf16[2048,512]{1,0:T(8,128)(2,1)S(1)}, bf16[2048,512]{1,0:T(8,128)(2,1)}, u32[]{:S(2)}) copy-start(bf16[2048,512]{1,0:T(8,128)(2,1)} %modes_ref.1) | copy-start | bytes 6291460
  2.9 1.2 %copy-start.1 = (bf16[32,128,128]{2,1,0:T(8,128)(2,1)S(1)}, bf16[32,128,128]{2,1,0:T(8,128)(2,1)}, u32[]{:S(2)}) copy-start(bf16[32,128,128]{2,1,0:T(8,128)(2,1)} %coupling_ref.1) | copy-start | bytes 3145732
  4.1 0.7 %copy-start.3 = (s32[32,128]{1,0:T(8,128)S(1)}, s32[32,128]{1,0:T(8,128)}, u32[]{:S(2)}) copy-start(s32[32,128]{1,0:T(8,128)} %offset_ref.1) | copy-start | bytes 49156
  4.8 0.7 %copy-start.4 = (f32[1,512]{1,0:T(1,128)S(1)}, f32[1,512]{1,0:T(1,128)}, u32[]{:S(2)}) copy-start(f32[1,512]{1,0:T(1,128)} %eig_ref.1) | copy-start | bytes 6148
  5.5 0.7 %copy-start.5 = (s32[32]{0:T(128)S(1)}, s32[32]{0:T(128)}, u32[]{:S(2)}) copy-start(s32[32]{0:T(128)} %spot_ref.3) | copy-start | bytes 388
  18.8 0.8 %copy-start.2 = (f32[1,128,128]{2,1,0:T(8,128)S(1)}, f32[1,128,128]{2,1,0:T(8,128)}, u32[]{:S(2)}) copy-start(f32[1,128,128]{2,1,0:T(8,128)} %iface_ref.1) | copy-start | bytes 196612
  19.6 0.7 %copy-start.6 = (f32[1,128]{1,0:T(1,128)S(1)}, f32[1,128]{1,0:T(1,128)}, u32[]{:S(2)}) copy-start(f32[1,128]{1,0:T(1,128)} %lumped_ref.1) | copy-start | bytes 1540

commit v4 on v3

--- a/solution.py
+++ b/solution.py
@@ -255,6 +255,7 @@
     blocks, depth, width = stiff_coupling.shape
     most, count = modes.shape
     f32, bf16 = jnp.float32, jnp.bfloat16
+    in_hbm = lambda x: pltpu.with_memory_space_constraint(x, pltpu.HBM)
     full = lambda *shape: pl.BlockSpec(shape, lambda i, *_: (0,) * len(shape))
     projected, stiff, mass = pl.pallas_call(
         project_kernel,
@@ -291,7 +292,7 @@
             dimension_semantics=("arbitrary",), vmem_limit_bytes=20 * MIB
         ),
         name="project",
-    )(sub_size, iface_offset, row_offset, modes, eigenvalues, stiff_coupling)
+    )(sub_size, in_hbm(iface_offset), *map(in_hbm, (row_offset, modes, eigenvalues, stiff_coupling)))
 
     vmem = pl.BlockSpec(memory_space=pltpu.VMEM)
     reduced, factor, near = pl.pallas_call(
@@ -318,7 +319,7 @@
             collective_id=0, has_side_effects=True, vmem_limit_bytes=8 * MIB
         ),
         name="exchange",
-    )(stiff, mass, stiff_iface, lumped_mass)
+    )(stiff, mass, in_hbm(stiff_iface), in_hbm(lumped_mass))
 
     coupled, reduced, factor = pl.pallas_call(
         couple_kernel,
@@ -346,7 +347,7 @@
             dimension_semantics=("arbitrary",), vmem_limit_bytes=12 * MIB
         ),
         name="couple",
-    )(iface_offset, projected, near, reduced, factor)
+    )(in_hbm(iface_offset), projected, near, reduced, factor)
     return reduced, factor, coupled
 
 

time: 51.1 us -> 47.6 us (0.932)
  local copies, waits for them, and re-layouts: 6.35 us -> 0 us
  Pallas kernels: 43.1 us -> 46 us
    unnamed x14 -> x0, local copies, waits for them, and re-layouts: 6.35 us -> none
    pallas_call x1, Pallas kernels: 12.6 us -> 14.5 us  [per_device(): pl.pallas_call(project_kernel, grid_spec=pltpu.PrefetchScalarGridSpec(num...]
    pallas_call x1, Pallas kernels: 24.6 us -> 25.4 us  [per_device(): pl.pallas_call(exchange_kernel, in_specs=[pl.BlockSpec(memory_space=pl.AN...]
where the time goes in v4:
time: 47.6 us; the launch traced here: 47.3 us
  Pallas kernels  46 us (97%)
  between operations  1.29 us (3%)
    pallas_call x1, Pallas kernels, per_device(): pl.pallas_call(exchange_kernel, in_specs=[pl.BlockSpec(memory_space=pl.AN...  25.4 us
    pallas_call x1, Pallas kernels, per_device(): pl.pallas_call(project_kernel, grid_spec=pltpu.PrefetchScalarGridSpec(num...  14.5 us
    pallas_call x1, Pallas kernels, per_device(): pl.pallas_call(couple_kernel, grid_spec=pltpu.PrefetchScalarGridSpec(num_...  6.08 us

profile of v4, /device:TPU:0, one launch (start us, length us, event | category | flops | bytes accessed | tf_op | source)
XLA Modules:
  0.0 47.3 jit_solution(4158967717680558008)
XLA Ops:
  1.3 14.5 %project.1 = (bf16[32,512,128]{2,1,0:T(8,128)(2,1)S(1)}, f32[7,128,128]{2,1,0:T(8,128)S(1)}, f32[7,72,128]{2,1,0:T(8,128)S(1)}) custom-call(s32[1]{0:T(128)S(6)} %copy.11.size_ref, s32[32]{0:T(128)} %spot_ref.3, s32[32,128]{1,0:T(8,128)} %offset_ref.1, bf16[2048,512]{1,0:T(8,128)(2,1)} %modes_ref.1, f32[1,512]{1,0:T(1,128)} %eig_ref.1, ...), custom_call_target="tpu_custom_call" | custom-call | tf_op jit(solution)/shard_map/project/pallas_call | solution.py:260
  15.8 25.4 %exchange.1 = (f32[128,128]{1,0:T(8,128)S(1)}, f32[128,128]{1,0:T(8,128)S(1)}, bf16[7,128,256]{2,1,0:T(8,128)(2,1)S(1)}) custom-call(f32[7,128,128]{2,1,0:T(8,128)S(1)} %get-tuple-element.13.stiff_ref, f32[7,72,128]{2,1,0:T(8,128)S(1)} %get-tuple-element.14.mass_ref, f32[1,128,128]{2,1,0:T(8,128)} %iface_ref.1, f32[1,128]{1,0:T(1,128)} %lumped_ref.1), custom_call_target="tpu_custom_call" | custom-call | tf_op jit(solution)/shard_map/exchange/pallas_call | solution.py:298
  41.3 6.1 %couple.1 = (bf16[32,512,128]{2,1,0:T(8,128)(2,1)}, f32[1,128,128]{2,1,0:T(8,128)}, f32[1,128,128]{2,1,0:T(8,128)}) custom-call(s32[32]{0:T(128)} %spot_ref.3, bf16[32,512,128]{2,1,0:T(8,128)(2,1)S(1)} %get-tuple-element.12.projected_ref, bf16[7,128,256]{2,1,0:T(8,128)(2,1)S(1)} %get-tuple-element.15.near_ref, f32[128,128]{1,0:T(8,128)S(1)} %get-tuple-element.16.reduced_in, ...), custom_call_target="tpu_custom_call" | custom-call | tf_op jit(solution)/shard_map/couple/pallas_call | solution.py:324

commit v5 on v4

--- a/solution.py
+++ b/solution.py
@@ -220,16 +220,17 @@
     for copy in mass_copies + stiff_copies:
         copy.wait_send()
 
-    def place(slot, x):
+    def place(slot, part, x):
         high, low = in_two(x)
-        near_ref[slot, :, :width] = high
-        near_ref[slot, :, width:] = low
-
-    place(REACH, own_ref[...])
-    for copy in near_copies:
-        copy.wait()
-    for d in others:
-        place(d + REACH, near_in[d + REACH])
+        near_ref[slot, part, :width] = high
+        near_ref[slot, part, width:] = low
+
+    place(REACH, pl.ds(0, width), own_ref[...])
+    for piece in range(PIECES):
+        part = pl.ds(piece * rows, rows)
+        for d, copy in zip(others, near_copies[piece * len(others):(piece + 1) * len(others)]):
+            copy.wait()
+            place(d + REACH, part, near_in[d + REACH, part, :])
 
 
 def couple_kernel(

time: 47.6 us -> 47.5 us (level)
  no operation moved by 1% of the time
where the time goes in v5:
time: 47.5 us; the launch traced here: 47.3 us
  Pallas kernels  46 us (97%)
  between operations  1.29 us (3%)
    pallas_call x1, Pallas kernels, per_device(): pl.pallas_call(exchange_kernel, in_specs=[pl.BlockSpec(memory_space=pl.AN...  25.4 us
    pallas_call x1, Pallas kernels, per_device(): pl.pallas_call(project_kernel, grid_spec=pltpu.PrefetchScalarGridSpec(num...  14.5 us
    pallas_call x1, Pallas kernels, per_device(): pl.pallas_call(couple_kernel, grid_spec=pltpu.PrefetchScalarGridSpec(num_...  6.08 us

profile of v5, /device:TPU:0, one launch (start us, length us, event | category | flops | bytes accessed | tf_op | source)
XLA Modules:
  0.0 47.3 jit_solution(4590975108121664117)
XLA Ops:
  1.3 14.5 %project.1 = (bf16[32,512,128]{2,1,0:T(8,128)(2,1)S(1)}, f32[7,128,128]{2,1,0:T(8,128)S(1)}, f32[7,72,128]{2,1,0:T(8,128)S(1)}) custom-call(s32[1]{0:T(128)S(6)} %copy.11.size_ref, s32[32]{0:T(128)} %spot_ref.3, s32[32,128]{1,0:T(8,128)} %offset_ref.1, bf16[2048,512]{1,0:T(8,128)(2,1)} %modes_ref.1, f32[1,512]{1,0:T(1,128)} %eig_ref.1, ...), custom_call_target="tpu_custom_call" | custom-call | tf_op jit(solution)/shard_map/project/pallas_call | solution.py:261
  15.8 25.4 %exchange.1 = (f32[128,128]{1,0:T(8,128)S(1)}, f32[128,128]{1,0:T(8,128)S(1)}, bf16[7,128,256]{2,1,0:T(8,128)(2,1)S(1)}) custom-call(f32[7,128,128]{2,1,0:T(8,128)S(1)} %get-tuple-element.13.stiff_ref, f32[7,72,128]{2,1,0:T(8,128)S(1)} %get-tuple-element.14.mass_ref, f32[1,128,128]{2,1,0:T(8,128)} %iface_ref.1, f32[1,128]{1,0:T(1,128)} %lumped_ref.1), custom_call_target="tpu_custom_call" | custom-call | tf_op jit(solution)/shard_map/exchange/pallas_call | solution.py:299
  41.2 6.1 %couple.1 = (bf16[32,512,128]{2,1,0:T(8,128)(2,1)}, f32[1,128,128]{2,1,0:T(8,128)}, f32[1,128,128]{2,1,0:T(8,128)}) custom-call(s32[32]{0:T(128)} %spot_ref.3, bf16[32,512,128]{2,1,0:T(8,128)(2,1)S(1)} %get-tuple-element.12.projected_ref, bf16[7,128,256]{2,1,0:T(8,128)(2,1)S(1)} %get-tuple-element.15.near_ref, f32[128,128]{1,0:T(8,128)S(1)} %get-tuple-element.16.reduced_in, ...), custom_call_target="tpu_custom_call" | custom-call | tf_op jit(solution)/shard_map/couple/pallas_call | solution.py:325
